TPU v7x, 32 devices: a whole 2x2x4 slice. The times are simulated.
32 devices in a mesh: seq: 2 (over x), tensor: 4 (over y, core), dp: 4 (over z).
Axes of the slice: x: 2, y: 2, z: 4, core: 2. Of those that a mesh axis runs over, the one named last changes fastest.
Arguments:
- inputs: bfloat16 [4, 512, 3584], P('dp', 'seq'), may hold values from -6 to 6
- w_query: bfloat16 [3584, 2048], P(('seq', 'dp'), 'tensor'), may hold values from -0.09375 to 0.09375
- w_key: bfloat16 [3584, 1024], P(('seq', 'dp'), 'tensor'), may hold values from -0.09375 to 0.09375
- w_value: bfloat16 [3584, 1024], P(('seq', 'dp'), 'tensor'), may hold values from -0.09375 to 0.09375
- norm_gain: float32 [3584], replicated, may hold values from 0.1 to 1.9
- attn_grad: bfloat16 [4, 512, 2048], P('dp', 'seq', 'tensor'), may hold values from -200 to 200
Outputs:
- grad_query: float32 [3584, 2048], P(('seq', 'dp'), 'tensor')
- grad_key: float32 [3584, 1024], P(('seq', 'dp'), 'tensor')
- grad_value: float32 [3584, 1024], P(('seq', 'dp'), 'tensor')
- input_grad: bfloat16 [4, 512, 3584], P('dp', 'seq', 'tensor')
All inputs are finite; a program needn't handle non-finite values.
Results may differ from a plain program's by a relative error of at most 0.01.
Values may be sent and summed in bfloat16 or wider, within the bound.
A program may use at most 64 MiB of HBM per device.

v0:
```python
import functools
import math

import jax
import jax.numpy as jnp
from jax import lax
from jax.experimental import pallas as pl
from jax.experimental.pallas import tpu as pltpu
from jax.sharding import PartitionSpec as P

D = 3584
H = 8
KVH = 4
HD = 256
WINDOW = 256


EPSILON = 1e-06
SOFTCAP = 50.0
CLIP_BOUND = 1.0
ROPE_BASE = 10000.0


def angles(positions, head_width):
    frequency = ROPE_BASE ** (-2.0 * jnp.arange(head_width // 2).astype(jnp.float32) / head_width)
    phases = positions.astype(jnp.float32)[:, None] * frequency[None, :]
    return (jnp.cos(phases)[:, None, :], jnp.sin(phases)[:, None, :])


MESH = pl.DeviceIdType.MESH


def greet(axes, peers=()):
    barrier = pltpu.get_barrier_semaphore()
    for axis in axes:
        count = lax.axis_size(axis)
        me = lax.axis_index(axis)
        for step in (1, -1):

            @pl.when((me + step >= 0) & (me + step < count))
            def _():
                pl.semaphore_signal(
                    barrier, inc=1, device_id={axis: me + step}, device_id_type=MESH
                )

    for peer in peers:
        pl.semaphore_signal(barrier, inc=1, device_id=peer, device_id_type=MESH)
    near = len(peers)
    for axis in axes:
        me = lax.axis_index(axis)
        near = near + jnp.minimum(me, 1) + jnp.minimum(lax.axis_size(axis) - 1 - me, 1)
    pl.semaphore_wait(barrier, near)


class LineGather:
    def __init__(self, order, part, first, second, low, high, x_ref, out_ref, send_sem, recv_sem):
        self.order = order
        self.part, self.first, self.second = part, first, second
        self.rows = pl.ds(low, high - low)
        self.x_ref, self.out_ref = x_ref, out_ref
        self.send_sem, self.recv_sem = send_sem, recv_sem
        self.me = {axis: lax.axis_index(axis) for axis in (first, second)}
        self.count = {axis: lax.axis_size(axis) for axis in (first, second)}
        self.sends = []

    def slot(self, at):
        return self.out_ref.at[tuple(at[axis] for axis in self.order) + (self.rows,)]

    def copy(self, at, axis, step, own):
        way = (0 if axis == "seq" else 2) + (0 if step == 1 else 1)
        return pltpu.make_async_remote_copy(
            src_ref=self.x_ref.at[self.rows] if own else self.slot(at),
            dst_ref=self.slot(at),
            send_sem=self.send_sem.at[self.part, way, at["seq"], at["dp"]],
            recv_sem=self.recv_sem.at[self.part, at["seq"], at["dp"]],
            device_id={axis: self.me[axis] + step},
            device_id_type=MESH,
        )

    def inside(self, axis, value):
        return (value >= 0) & (value < self.count[axis])

    def send(self, at, axis, step, held, own=False):
        ok = held & self.inside(axis, self.me[axis] + step)

        @pl.when(ok)
        def _():
            self.copy(at, axis, step, own).start()

        self.sends.append((at, axis, step, ok, own))

    def receive(self, at, held):
        @pl.when(held)
        def _():
            self.copy(at, self.first, 1, False).wait_recv()

    def steps(self):
        first, second = self.first, self.second
        here = jnp.bool_(True)
        for axis in (first, second):
            for step in (1, -1):
                self.send(dict(self.me), axis, step, here, True)
        yield
        column = [(dict(self.me), here, True)]
        for hop in range(1, self.count[first]):
            for step in (1, -1):
                at = {**self.me, first: self.me[first] - step * hop}
                held = self.inside(first, at[first])
                self.receive(at, held)
                self.send(at, first, step, held)
                for way in (1, -1):
                    self.send(at, second, way, held)
                column.append((at, held, False))
            yield
        for hop in range(1, self.count[second]):
            for base, held_base, _ in column:
                for step in (1, -1):
                    at = {**base, second: self.me[second] - step * hop}
                    held = held_base & self.inside(second, at[second])
                    self.receive(at, held)
                    self.send(at, second, step, held)
            yield

    def finish(self):
        for at, axis, step, ok, own in self.sends:

            @pl.when(ok)
            def _():
                self.copy(at, axis, step, own).wait_send()


def run_gathers(gathers):
    live = [gather.steps() for gather in gathers]
    while live:
        still = []
        for walk in live:
            try:
                next(walk)
                still.append(walk)
            except StopIteration:
                pass
        live = still
    for gather in gathers:
        gather.finish()


def gather_kernel(cut, order, x_ref, out_ref, send_sem, recv_sem, own_sem):
    rows = x_ref.shape[0]
    own = pltpu.make_async_copy(
        x_ref, out_ref.at[tuple(lax.axis_index(axis) for axis in order)], own_sem
    )
    own.start()
    greet(("seq", "dp"))
    run_gathers(
        [
            LineGather(order, 0, "seq", "dp", 0, cut, x_ref, out_ref, send_sem, recv_sem),
            LineGather(order, 1, "dp", "seq", cut, rows, x_ref, out_ref, send_sem, recv_sem),
        ]
    )
    own.wait()


def gather_blocks(x, cut, order, collective_id):
    shape = (lax.axis_size("seq"), lax.axis_size("dp"))
    return pl.pallas_call(
        functools.partial(gather_kernel, cut, order),
        out_shape=jax.ShapeDtypeStruct(
            tuple(lax.axis_size(axis) for axis in order) + x.shape, x.dtype
        ),
        in_specs=[pl.BlockSpec(memory_space=pltpu.VMEM)],
        out_specs=pl.BlockSpec(memory_space=pl.ANY),
        scratch_shapes=[
            pltpu.SemaphoreType.DMA((2, 4) + shape),
            pltpu.SemaphoreType.DMA((2,) + shape),
            pltpu.SemaphoreType.DMA,
        ],
        compiler_params=pltpu.CompilerParams(
            collective_id=collective_id, has_side_effects=True
        ),
    )(x)


def tail_kernel(
    cut,
    order,
    x_ref,
    part_ref,
    inner_ref,
    block_ref,
    out_ref,
    parts_ref,
    inners_ref,
    blocks_ref,
    send_sem,
    recv_sem,
    own_sem,
    part_send,
    part_recv,
    inner_send,
    inner_recv,
    block_send,
    block_recv,
):
    rows = x_ref.shape[0]
    count, me = lax.axis_size("tensor"), lax.axis_index("tensor")
    width = part_ref.shape[1] // count

    def slab(index):
        return part_ref.at[:, pl.ds(pl.multiple_of(index * width, 128), width)]

    owns = [
        pltpu.make_async_copy(
            x_ref, out_ref.at[tuple(lax.axis_index(axis) for axis in order)], own_sem.at[0]
        ),
        pltpu.make_async_copy(slab(me), parts_ref.at[me], own_sem.at[1]),
        pltpu.make_async_copy(inner_ref, inners_ref.at[me], own_sem.at[2]),
        pltpu.make_async_copy(block_ref, blocks_ref.at[me], own_sem.at[3]),
    ]
    for own in owns:
        own.start()
    others = [lax.rem(me + hop, count) for hop in range(1, count)]
    greet(("seq", "dp"), [{"tensor": other} for other in others])
    copies = []
    for index, other in enumerate(others):
        copies.append(
            pltpu.make_async_remote_copy(
                src_ref=slab(other),
                dst_ref=parts_ref.at[me],
                send_sem=part_send.at[index],
                recv_sem=part_recv.at[index],
                device_id={"tensor": other},
                device_id_type=MESH,
            )
        )
        copies.append(
            pltpu.make_async_remote_copy(
                src_ref=inner_ref,
                dst_ref=inners_ref.at[me],
                send_sem=inner_send.at[index],
                recv_sem=inner_recv.at[index],
                device_id={"tensor": other},
                device_id_type=MESH,
            )
        )
    for index, other in enumerate(others):
        copies.append(
            pltpu.make_async_remote_copy(
                src_ref=block_ref,
                dst_ref=blocks_ref.at[me],
                send_sem=block_send.at[index],
                recv_sem=block_recv.at[index],
                device_id={"tensor": other},
                device_id_type=MESH,
            )
        )
    for copy in copies:
        copy.start()
    run_gathers(
        [
            LineGather(order, 0, "seq", "dp", 0, cut, x_ref, out_ref, send_sem, recv_sem),
            LineGather(order, 1, "dp", "seq", cut, rows, x_ref, out_ref, send_sem, recv_sem),
        ]
    )
    for copy in copies:
        copy.wait()
    for own in owns:
        own.wait()


def gather_and_scatter(x, part, inner, block, cut, order, collective_id):
    shape = (lax.axis_size("seq"), lax.axis_size("dp"))
    count = lax.axis_size("tensor")
    return pl.pallas_call(
        functools.partial(tail_kernel, cut, order),
        out_shape=(
            jax.ShapeDtypeStruct(tuple(lax.axis_size(axis) for axis in order) + x.shape, x.dtype),
            jax.ShapeDtypeStruct((count, part.shape[0], part.shape[1] // count), part.dtype),
            jax.ShapeDtypeStruct((count,) + inner.shape, inner.dtype),
            jax.ShapeDtypeStruct((count,) + block.shape, block.dtype),
        ),
        in_specs=[pl.BlockSpec(memory_space=pltpu.VMEM)] * 4,
        out_specs=(pl.BlockSpec(memory_space=pl.ANY),) * 4,
        scratch_shapes=[
            pltpu.SemaphoreType.DMA((2, 4) + shape),
            pltpu.SemaphoreType.DMA((2,) + shape),
            pltpu.SemaphoreType.DMA((4,)),
        ]
        + [pltpu.SemaphoreType.DMA((count - 1,))] * 6,
        compiler_params=pltpu.CompilerParams(
            collective_id=collective_id, has_side_effects=True
        ),
    )(x, part, inner, block)


def block_peers():
    seqs, dps = lax.axis_size("seq"), lax.axis_size("dp")
    mine = lax.axis_index("dp") * seqs + lax.axis_index("seq")
    others = [lax.rem(mine + hop, seqs * dps) for hop in range(1, seqs * dps)]
    return mine, [(other, lax.rem(other, seqs), other // seqs) for other in others]


def tensor_peers():
    count, me = lax.axis_size("tensor"), lax.axis_index("tensor")
    return [lax.rem(me + hop, count) for hop in range(1, count)]


class Exchange:
    def __init__(self, x_ref, out_ref, send_sem, recv_sem, own_sem):
        self.x_ref, self.out_ref = x_ref, out_ref
        self.send_sem, self.recv_sem, self.own_sem = send_sem, recv_sem, own_sem
        self.lanes, self.lane = lax.axis_size("tensor"), lax.axis_index("tensor")
        self.mine, self.peers = block_peers()
        self.sender = lax.rem(self.mine, self.lanes) == self.lane

    def copy(self, hop, slot):
        _, seq, dp = self.peers[hop]
        return pltpu.make_async_remote_copy(
            src_ref=self.x_ref.at[seq, dp],
            dst_ref=self.out_ref.at[slot],
            send_sem=self.send_sem.at[hop],
            recv_sem=self.recv_sem.at[slot],
            device_id={"seq": seq, "dp": dp},
            device_id_type=MESH,
        )

    def own(self):
        return pltpu.make_async_copy(
            self.x_ref.at[lax.axis_index("seq"), lax.axis_index("dp")],
            self.out_ref.at[self.mine // self.lanes],
            self.own_sem,
        )

    def start(self):
        @pl.when(self.sender)
        def _():
            for hop in range(len(self.peers)):
                self.copy(hop, self.mine // self.lanes).start()
            self.own().start()

    def finish(self):
        for slot in range((len(self.peers) + 1) // self.lanes):

            @pl.when(self.lane + slot * self.lanes != self.mine)
            def _():
                self.copy(0, slot).wait_recv()

        @pl.when(self.sender)
        def _():
            for hop in range(len(self.peers)):
                self.copy(hop, self.mine // self.lanes).wait_send()
            self.own().wait()


def exchange_semaphores():
    count, lanes = lax.axis_size("seq") * lax.axis_size("dp"), lax.axis_size("tensor")
    return [
        pltpu.SemaphoreType.DMA((count - 1,)),
        pltpu.SemaphoreType.DMA((count // lanes,)),
        pltpu.SemaphoreType.DMA,
    ]


def turn(vectors, cosine, sine_part, direction):
    half = vectors.shape[-1] // 2
    low, high = vectors[:, :half], vectors[:, half:]
    return jnp.concatenate(
        [
            low * cosine - direction * high * sine_part,
            high * cosine + direction * low * sine_part,
        ],
        -1,
    )


def product(left, right, left_dim, right_dim):
    return lax.dot_general(
        left, right, (((left_dim,), (right_dim,)), ((), ())), preferred_element_type=jnp.float32
    )


def attend_kernel(
    width_q,
    proj_ref,
    cos_ref,
    sin_ref,
    cot_ref,
    block_ref,
    out_ref,
    blocks_ref,
    held,
    before,
    back_out,
    back_in,
    own_grad,
    kv_sems,
    back_sems,
    *exchange_sems,
):
    rows = proj_ref.shape[0]
    width_k = (proj_ref.shape[1] - width_q) // 2
    heads_k = width_k // HD
    group = width_q // width_k
    inv_scale = 1.0 / math.sqrt(HD)
    seqs, seq = lax.axis_size("seq"), lax.axis_index("seq")
    cosine, sine_part = cos_ref[...], sin_ref[...]
    for head in range(heads_k):
        low = head * HD
        at = slice(low, low + HD)
        keys = proj_ref[:, width_q + low : width_q + low + HD]
        held[:, at] = turn(keys, cosine, sine_part, 1.0).astype(jnp.bfloat16)
        values = proj_ref[:, width_q + width_k + low : width_q + width_k + low + HD]
        held[:, width_k + low : width_k + low + HD] = values.astype(jnp.bfloat16)
    _, peers = block_peers()
    greet((), [{"seq": other, "dp": far} for _, other, far in peers])
    ahead = pltpu.make_async_remote_copy(
        src_ref=held,
        dst_ref=before,
        send_sem=kv_sems.at[0],
        recv_sem=kv_sems.at[1],
        device_id={"seq": seq + 1},
        device_id_type=MESH,
    )
    behind = pltpu.make_async_remote_copy(
        src_ref=back_out,
        dst_ref=back_in,
        send_sem=back_sems.at[0],
        recv_sem=back_sems.at[1],
        device_id={"seq": seq - 1},
        device_id_type=MESH,
    )
    has_next, has_last = seq < seqs - 1, seq > 0

    @pl.when(has_next)
    def _():
        ahead.start()

    exchange = Exchange(block_ref, blocks_ref, *exchange_sems)
    exchange.start()

    queries = []
    for head in range(heads_k * group):
        part = proj_ref[:, head * HD : (head + 1) * HD]
        queries.append(turn(part, cosine, sine_part, 1.0).astype(jnp.bfloat16))

    @pl.when(has_last)
    def _():
        ahead.wait_recv()

    @pl.when(jnp.logical_not(has_last))
    def _():
        before[...] = jnp.zeros_like(before)

    query_at = lax.broadcasted_iota(jnp.int32, (rows, rows), 0)
    key_at = lax.broadcasted_iota(jnp.int32, (rows, rows), 1)
    masks = (
        (key_at > query_at + (rows - WINDOW)) & (seq * rows - rows + key_at >= 0),
        (key_at <= query_at) & (key_at > query_at - WINDOW),
    )
    for head in range(heads_k):
        at = slice(head * HD, (head + 1) * HD)
        at_value = slice(width_k + head * HD, width_k + (head + 1) * HD)
        sides = (before, held)
        key_grads, value_grads = [0.0, 0.0], [0.0, 0.0]
        for member in range(group):
            index = head * group + member
            query = queries[index]
            cot = cot_ref[:, index * HD : (index + 1) * HD]
            squashes, terms, slopes = [], [], []
            for side, mask in zip(sides, masks):
                squash = jnp.tanh(product(query, side[:, at], 1, 1) * inv_scale / SOFTCAP)
                squashes.append(squash)
                terms.append(jnp.where(mask, jnp.exp(SOFTCAP * squash), 0.0))
                slopes.append(product(cot, side[:, at_value], 1, 1))
            total = sum(jnp.sum(term, -1, keepdims=True) for term in terms)
            probs = [term / total for term in terms]
            delta = sum(
                jnp.sum(prob * slope, -1, keepdims=True) for prob, slope in zip(probs, slopes)
            )
            dquery = 0.0
            for which in range(2):
                prob, squash = probs[which], squashes[which]
                dlogits = (
                    prob * (slopes[which] - delta) * (1.0 - squash * squash) * inv_scale
                ).astype(jnp.bfloat16)
                dquery = dquery + product(dlogits, sides[which][:, at], 1, 0)
                key_grads[which] = key_grads[which] + product(dlogits, query, 0, 0)
                value_grads[which] = value_grads[which] + product(
                    prob.astype(jnp.bfloat16), cot, 0, 0
                )
            out_ref[:, index * HD : (index + 1) * HD] = turn(
                dquery, cosine, sine_part, -1.0
            ).astype(jnp.bfloat16)
        back_out[:, at] = key_grads[0].astype(jnp.bfloat16)
        back_out[:, at_value] = value_grads[0].astype(jnp.bfloat16)
        own_grad[:, at] = key_grads[1]
        own_grad[:, at_value] = value_grads[1]

    @pl.when(has_last)
    def _():
        behind.start()

    @pl.when(has_next)
    def _():
        behind.wait_recv()
        own_grad[...] += back_in[...].astype(jnp.float32)

    for head in range(heads_k):
        at = slice(head * HD, (head + 1) * HD)
        out_ref[:, width_q + head * HD : width_q + (head + 1) * HD] = turn(
            own_grad[:, at], cosine, sine_part, -1.0
        ).astype(jnp.bfloat16)
    out_ref[:, width_q + width_k :] = own_grad[:, width_k:].astype(jnp.bfloat16)

    @pl.when(has_next)
    def _():
        ahead.wait_send()

    @pl.when(has_last)
    def _():
        behind.wait_send()

    exchange.finish()


def attend_and_exchange(projected, cosine, sine_part, cotangent, blocks, collective_id):
    rows, width_q = cotangent.shape
    width_k = (projected.shape[1] - width_q) // 2
    return pl.pallas_call(
        functools.partial(attend_kernel, width_q),
        out_shape=(
            jax.ShapeDtypeStruct(projected.shape, jnp.bfloat16),
            jax.ShapeDtypeStruct(
                (blocks.shape[0] * blocks.shape[1] // lax.axis_size("tensor"),)
                + blocks.shape[2:],
                blocks.dtype,
            ),
        ),
        in_specs=[pl.BlockSpec(memory_space=pltpu.VMEM)] * 5,
        out_specs=(pl.BlockSpec(memory_space=pltpu.VMEM), pl.BlockSpec(memory_space=pl.ANY)),
        scratch_shapes=[
            pltpu.VMEM((rows, 2 * width_k), jnp.bfloat16),
            pltpu.VMEM((rows, 2 * width_k), jnp.bfloat16),
            pltpu.VMEM((rows, 2 * width_k), jnp.bfloat16),
            pltpu.VMEM((rows, 2 * width_k), jnp.bfloat16),
            pltpu.VMEM((rows, 2 * width_k), jnp.float32),
            pltpu.SemaphoreType.DMA((2,)),
            pltpu.SemaphoreType.DMA((2,)),
        ]
        + exchange_semaphores(),
        compiler_params=pltpu.CompilerParams(
            collective_id=collective_id, has_side_effects=True
        ),
    )(projected, cosine, sine_part, cotangent, blocks)


def total_kernel(x_ref, out_ref, held, send_sem, recv_sem, send_wide, recv_wide, own_sem):
    mine, peers = block_peers()
    lane = lax.axis_index("tensor")
    others = tensor_peers()
    own = pltpu.make_async_copy(x_ref, held.at[lane, mine], own_sem)
    own.start()
    greet(
        (),
        [{"seq": seq, "dp": dp} for _, seq, dp in peers] + [{"tensor": other} for other in others],
    )
    near = [
        pltpu.make_async_remote_copy(
            src_ref=x_ref,
            dst_ref=held.at[lane, mine],
            send_sem=send_sem.at[hop],
            recv_sem=recv_sem.at[mine],
            device_id={"seq": seq, "dp": dp},
            device_id_type=MESH,
        )
        for hop, (_, seq, dp) in enumerate(peers)
    ]
    for copy in near:
        copy.start()
    for index, seq, dp in peers:
        pltpu.make_async_remote_copy(
            src_ref=x_ref,
            dst_ref=held.at[lane, index],
            send_sem=send_sem.at[0],
            recv_sem=recv_sem.at[index],
            device_id={"seq": seq, "dp": dp},
            device_id_type=MESH,
        ).wait_recv()
    own.wait()
    far = [
        pltpu.make_async_remote_copy(
            src_ref=held.at[lane],
            dst_ref=held.at[lane],
            send_sem=send_wide.at[hop],
            recv_sem=recv_wide.at[hop],
            device_id={"tensor": other},
            device_id_type=MESH,
        )
        for hop, other in enumerate(others)
    ]
    for copy in far:
        copy.start()
    for copy in far:
        copy.wait()
    for copy in near:
        copy.wait_send()
    out_ref[...] = jnp.sum(held[...], (0, 1))


def total_of(x, collective_id):
    count, lanes = lax.axis_size("seq") * lax.axis_size("dp"), lax.axis_size("tensor")
    return pl.pallas_call(
        total_kernel,
        out_shape=jax.ShapeDtypeStruct(x.shape, x.dtype),
        in_specs=[pl.BlockSpec(memory_space=pltpu.VMEM)],
        out_specs=pl.BlockSpec(memory_space=pltpu.VMEM),
        scratch_shapes=[
            pltpu.VMEM((lanes, count) + x.shape, x.dtype),
            pltpu.SemaphoreType.DMA((count - 1,)),
            pltpu.SemaphoreType.DMA((count,)),
            pltpu.SemaphoreType.DMA((lanes - 1,)),
            pltpu.SemaphoreType.DMA((lanes - 1,)),
            pltpu.SemaphoreType.DMA,
        ],
        compiler_params=pltpu.CompilerParams(
            collective_id=collective_id, has_side_effects=True
        ),
    )(x)


def cut_of(rows):
    return max(16, rows // 7 // 16 * 16)


def local(inputs, w_query, w_key, w_value, norm_gain, attn_grad):
    widened = inputs[0].astype(jnp.float32)
    row_count = widened.shape[0]
    inverse_rms = lax.rsqrt(jnp.mean(widened * widened, -1) + EPSILON)
    normed = (widened * inverse_rms[:, None] * norm_gain[None, :]).astype(jnp.bfloat16)
    width_q = w_query.shape[1]
    width_k = w_key.shape[1]
    local_w = jnp.concatenate([w_query, w_key, w_value], 1)
    seqs, dps = lax.axis_size("seq"), lax.axis_size("dp")
    rows_w = local_w.shape[0]
    full_w = gather_blocks(local_w, cut_of(rows_w), ("seq", "dp"), 0)
    full_w = full_w.reshape(seqs * dps * rows_w, -1)
    projected = jnp.dot(normed, full_w, preferred_element_type=jnp.float32)
    start_row = lax.axis_index("seq") * row_count
    cosine, sine_part = angles(start_row + jnp.arange(row_count, dtype=jnp.int32), HD)
    d_out, passed = attend_and_exchange(
        projected,
        cosine[:, 0],
        sine_part[:, 0],
        attn_grad[0],
        normed.T.reshape(seqs, dps, rows_w, row_count),
        3,
    )
    dnormed = lax.dot_general(
        d_out, full_w, (((1,), (1,)), ((), ())), preferred_element_type=jnp.float32
    )
    inner = jnp.sum(widened * norm_gain[None, :] * dnormed, -1).reshape(-1, 128)
    cotangents, parts, inners, slabs = gather_and_scatter(
        d_out, dnormed.astype(jnp.bfloat16), inner, passed, cut_of(row_count), ("dp", "seq"), 2
    )
    grads = []
    lanes = lax.axis_size("tensor")
    for example in range(dps):
        grads.append(
            sum(
                jnp.dot(
                    slabs[(example * seqs + s) % lanes, (example * seqs + s) // lanes],
                    cotangents[example, s],
                    preferred_element_type=jnp.float32
                )
                for s in range(seqs)
            )
        )
    squares = jnp.stack([jnp.sum(grad * grad) for grad in grads])
    square_sum = total_of(jnp.broadcast_to(squares[:, None], (dps, 128)), 1)[:, 0]
    grad_rms = jnp.sqrt(square_sum / (D * (H + 2 * KVH) * HD) + EPSILON)
    factor = CLIP_BOUND / jnp.maximum(grad_rms, CLIP_BOUND)
    clipped = sum(factor[example] * grads[example] for example in range(dps))
    part_width = D // lax.axis_size("tensor")
    offset = lax.axis_index("tensor") * part_width
    part_grad = jnp.sum(parts.astype(jnp.float32), 0)
    gain_slab = lax.dynamic_slice_in_dim(norm_gain, offset, part_width, 0)
    input_slab = lax.dynamic_slice_in_dim(widened, offset, part_width, 1)
    scaled = gain_slab[None, :] * part_grad
    inner_sum = jnp.sum(inners, 0).reshape(row_count)
    mean_term = (inner_sum / D)[:, None]
    input_grad = (
        inverse_rms[:, None] * scaled
        - input_slab * (inverse_rms * inverse_rms * inverse_rms)[:, None] * mean_term
    )
    return (
        clipped[:, :width_q],
        clipped[:, width_q : width_q + width_k],
        clipped[:, width_q + width_k :],
        input_grad.astype(jnp.bfloat16)[None],
    )


def solution(mesh):
    return jax.shard_map(
        local,
        mesh=mesh,
        in_specs=(
            P("dp", "seq", None),
            P(("seq", "dp"), "tensor"),
            P(("seq", "dp"), "tensor"),
            P(("seq", "dp"), "tensor"),
            P(),
            P("dp", "seq", "tensor"),
        ),
        out_specs=(
            P(("seq", "dp"), "tensor"),
            P(("seq", "dp"), "tensor"),
            P(("seq", "dp"), "tensor"),
            P("dp", "seq", "tensor"),
        ),
        check_vma=False,
    )
```

profile of v0, /device:TPU:0, one launch (start us, length us, event | category | flops | bytes accessed | tf_op | source)
XLA Modules:
  0.0 223.3 jit_solution(15125711788191159381)
XLA Ops:
  0.6 0.0 copy-start.3
  0.6 0.0 copy-start.5
  0.7 0.0 copy-start.4
  0.7 2.0 fusion
  2.7 0.0 copy-done.3
  2.7 0.0 copy-done.5
  2.7 0.0 copy-done.4
  2.7 1.0 pad_maximum_fusion.x_ref
  3.8 0.0 copy-start
  3.8 0.0 copy-start.6
  3.8 86.9 %shard_map.93 = bf16[2,4,448,1024]{3,2,1,0:T(8,128)(2,1)} custom-call(bf16[448,1024]{1,0:T(8,128)(2,1)} %pad_maximum_fusion.x_ref), custom_call_target="tpu_custom_call" | custom-call | tf_op jit(solution)/shard_map/pallas_call | solution.py:165
  90.6 0.0 copy-done
  90.6 0.0 copy-done.6
  90.6 6.2 %fusion.6.proj_ref = f32[256,1024]{1,0:T(8,128)} fusion(bf16[3584,1024]{1,0:T(8,128)(2,1)} %bitcast.115, bf16[1,256,3584]{2,1,0:T(8,128)(2,1)S(1)} %copy-done, f32[3584]{0:T(1024)S(1)} %copy-done.6, f32[256]{0:T(256)S(1)} %get-tuple-element.27), kind=kOutput, calls=%fused_computation.11 | convolution fusion | flops 1882718208 | bytes 10238976 | tf_op jit(solution)/shard_map/dot_general | solution.py:646
  96.8 1.8 fusion.8
  98.6 3.8 %copy.10 = bf16[3584,256]{1,0:T(8,128)(2,1)} copy(bf16[3584,256]{0,1:T(8,128)(2,1)} %fusion.8) | data formatting | bytes 3670016 | tf_op jit(solution)/shard_map/transpose | solution.py:654
  102.4 1.2 multiply_sine_fusion
  103.7 21.9 %shard_map.94 = (bf16[256,1024]{1,0:T(8,128)(2,1)}, bf16[2,448,256]{2,1,0:T(8,128)(2,1)}) custom-call(f32[256,1024]{1,0:T(8,128)} %fusion.6.proj_ref, f32[256,128]{1,0:T(8,128)} %get-tuple-element.25.cos_ref, f32[256,128]{1,0:T(8,128)} %get-tuple-element.24.sin_ref, bf16[256,512]{1,0:T(8,128)(2,1)} %bitcast.117, bf16[2,4,448,256]{3,2,1,0:T(8,128)(2,1)} %bitcast.114), custom_call_target="tpu_custom_call" | custom-call | tf_op jit(solution)/shard_map/pallas_call | solution.py:528
  125.6 7.3 %fusion.4 = (f32[256]{0:T(256)}, bf16[256,3584]{1,0:T(8,128)(2,1)}) fusion(bf16[1,256,3584]{2,1,0:T(8,128)(2,1)S(1)} %copy-done, f32[3584]{0:T(1024)S(1)} %copy-done.6, bf16[256,1024]{1,0:T(8,128)(2,1)} %get-tuple-element.10.x_ref, bf16[3584,1024]{1,0:T(8,128)(2,1)} %bitcast.116), kind=kOutput, calls=%fused_computation.7 | convolution fusion | flops 1883635456 | bytes 11549696 | tf_op jit(solution)/shard_map/dot_general | solution.py:657
  132.9 51.7 %shard_map.95 = (bf16[4,2,256,1024]{3,2,1,0:T(8,128)(2,1)}, bf16[4,256,896]{2,1,0:T(8,128)(2,1)}, f32[4,2,128]{2,1,0:T(2,128)}, bf16[4,2,448,256]{3,2,1,0:T(8,128)(2,1)}) custom-call(bf16[256,1024]{1,0:T(8,128)(2,1)} %get-tuple-element.10.x_ref, bf16[256,3584]{1,0:T(8,128)(2,1)} %get-tuple-element.17.part_ref, f32[2,128]{1,0:T(2,128)} %bitcast.118, ...), custom_call_target="tpu_custom_call" | custom-call | tf_op jit(solution)/shard_map/pallas_call | solution.py:273
  184.7 0.0 copy-start.7
  184.7 1.8 convert_reduce_fusion
  186.5 0.0 copy-done.7
  186.6 0.1 dynamic_slice.8
  186.7 0.0 copy-start.1
  186.7 0.4 convert_element_type.38
  187.1 0.0 copy-start.2
  187.1 1.0 fusion.34
  188.1 0.9 copy-done.1
  189.0 0.7 copy-done.2
  189.7 0.4 fusion.24
  190.1 1.2 multiply_reduce_fusion.3
  191.3 0.4 fusion.21
  191.7 2.4 %multiply_reduce_fusion.2 = (f32[]{:T(128)}, f32[448,1024]{1,0:T(8,128)}) fusion(f32[448,1024]{1,0:T(8,128)S(1)} %fusion.21, bf16[4,2,256,1024]{3,2,1,0:T(8,128)(2,1)S(1)} %copy-done.1, bf16[4,2,448,256]{3,2,1,0:T(8,128)(2,1)S(1)} %copy-done.2), kind=kOutput, calls=%fused_computation.16 | convolution fusion | flops 236257280 | bytes 4423684 | tf_op jit(solution)/shard_map/dot_general | solution.py:669
  194.2 0.4 fusion.18
  194.6 2.4 %multiply_reduce_fusion.1 = (f32[]{:T(128)}, f32[448,1024]{1,0:T(8,128)}) fusion(f32[448,1024]{1,0:T(8,128)S(1)} %fusion.18, bf16[4,2,256,1024]{3,2,1,0:T(8,128)(2,1)S(1)} %copy-done.1, bf16[4,2,448,256]{3,2,1,0:T(8,128)(2,1)S(1)} %copy-done.2), kind=kOutput, calls=%fused_computation.15 | convolution fusion | flops 236257280 | bytes 4423684 | tf_op jit(solution)/shard_map/dot_general | solution.py:669
  197.0 0.4 fusion.15
  197.4 2.4 %multiply_reduce_fusion = (f32[]{:T(128)}, f32[448,1024]{1,0:T(8,128)}) fusion(f32[448,1024]{1,0:T(8,128)S(1)} %fusion.15, bf16[4,2,256,1024]{3,2,1,0:T(8,128)(2,1)S(1)} %copy-done.1, bf16[4,2,448,256]{3,2,1,0:T(8,128)(2,1)S(1)} %copy-done.2), kind=kOutput, calls=%fused_computation.14 | convolution fusion | flops 236257280 | bytes 4423684 | tf_op jit(solution)/shard_map/dot_general | solution.py:669
  199.8 2.6 %pad_maximum_fusion.1 = f32[4]{0:T(128)S(1)} fusion(f32[1]{0:T(128)} %bitcast.26, f32[1]{0:T(128)} %bitcast.21, f32[1]{0:T(128)} %bitcast.16, f32[1]{0:T(128)} %bitcast.11), kind=kLoop, calls=%fused_computation.73 | loop fusion | flops 12 | bytes 32 | tf_op jit(solution)/shard_map/stack | solution.py:677
  202.4 0.7 broadcast_in_dim.4.x_ref
  203.0 11.1 %shard_map.96 = f32[4,128]{1,0:T(4,128)} custom-call(f32[4,128]{1,0:T(4,128)} %broadcast_in_dim.4.x_ref), custom_call_target="tpu_custom_call" | custom-call | tf_op jit(solution)/shard_map/pallas_call | solution.py:611
  214.1 0.7 maximum_divide_fusion
  214.8 0.5 fusion.52
  215.4 5.9 %multiply_add_fusion = f32[448,1024]{1,0:T(8,128)S(1)} fusion(f32[448,1024]{1,0:T(8,128)} %get-tuple-element.30, f32[448,1024]{1,0:T(8,128)} %get-tuple-element.32, f32[448,1024]{1,0:T(8,128)} %get-tuple-element.34, f32[448,1024]{1,0:T(8,128)S(1)} %get-tuple-element.36, f32[]{:T(128)} %bitcast.30, f32[]{:T(128)} %bitcast.29, f32[]{:T(128)} %bitcast.28, ...), kind=kLoop, calls=%fused_computation.13 | loop fusion | flops 3211264 | bytes 9175056 | tf_op jit(solution)/shard_map/add | solution.py:681
  221.3 1.0 fusion.51
  222.3 1.0 slice.100
  (5 shorter events, 0.0 us)
Async XLA Ops:
  0.6 2.1 copy-start.3
  0.6 2.1 copy-start.5
  0.7 2.1 copy-start.4
  3.8 86.9 %copy-start = (bf16[1,256,3584]{2,1,0:T(8,128)(2,1)S(1)}, bf16[1,256,3584]{2,1,0:T(8,128)(2,1)}, u32[]{:S(2)}) copy-start(bf16[1,256,3584]{2,1,0:T(8,128)(2,1)} %param.6) | copy-start | bytes 5505028
  3.8 86.9 %copy-start.6 = (f32[3584]{0:T(1024)S(1)}, f32[3584]{0:T(1024)}, u32[]{:S(2)}) copy-start(f32[3584]{0:T(1024)} %param.10) | copy-start | bytes 43012
  184.7 1.9 copy-start.7
  186.7 2.4 %copy-start.1 = (bf16[4,2,256,1024]{3,2,1,0:T(8,128)(2,1)S(1)}, bf16[4,2,256,1024]{3,2,1,0:T(8,128)(2,1)}, u32[]{:S(2)}) copy-start(bf16[4,2,256,1024]{3,2,1,0:T(8,128)(2,1)} %get-tuple-element.13) | copy-start | bytes 12582916
  187.1 2.6 %copy-start.2 = (bf16[4,2,448,256]{3,2,1,0:T(8,128)(2,1)S(1)}, bf16[4,2,448,256]{3,2,1,0:T(8,128)(2,1)}, u32[]{:S(2)}) copy-start(bf16[4,2,448,256]{3,2,1,0:T(8,128)(2,1)} %get-tuple-element.12) | copy-start | bytes 5505028
where the time goes:
time: 224 us; the launch traced here: 223 us
  Pallas kernels  172 us (77%)
  matrix products  23.6 us (11%)
  other arithmetic  18.6 us (8%)
  local copies, waits for them, and re-layouts  8.73 us (4%)
    pallas_call x1, Pallas kernels, gather_blocks(): pl.pallas_call(functools.partial(gather_kernel, cut, order), out_shape=ja...  86.9 us
    pallas_call x1, Pallas kernels, gather_and_scatter(): pl.pallas_call(functools.partial(tail_kernel, cut, order), out_shape=(jax...  51.7 us
    pallas_call x1, Pallas kernels, attend_and_exchange(): pl.pallas_call(functools.partial(attend_kernel, width_q), out_shape=(jax....  21.9 us
    pallas_call x1, Pallas kernels, total_of(): pl.pallas_call(total_kernel, out_shape=jax.ShapeDtypeStruct(x.shape, x.dt...  11.1 us
    dot_general x8, matrix products, local(): jnp.dot(slabs[(example * seqs + s) % lanes, (example * seqs + s) // lanes...  10.1 us
    dot_general x1, matrix products, local(): lax.dot_general(d_out, full_w, (((1,), (1,)), ((), ())), preferred_elemen...  7.33 us
    dot_general x1, matrix products, local(): projected = jnp.dot(normed, full_w, preferred_element_type=jnp.float32)  6.16 us
    add x1, other arithmetic, local(): clipped = sum((factor[example] * grads[example] for example in range(dps)))  5.95 us

commit v1 on v0

--- a/solution.py
+++ b/solution.py
@@ -631,7 +631,7 @@
     return max(16, rows // 7 // 16 * 16)
 
 
-def local(inputs, w_query, w_key, w_value, norm_gain, attn_grad):
+def gathered_local(inputs, w_query, w_key, w_value, norm_gain, attn_grad):
     widened = inputs[0].astype(jnp.float32)
     row_count = widened.shape[0]
     inverse_rms = lax.rsqrt(jnp.mean(widened * widened, -1) + EPSILON)
@@ -699,6 +699,932 @@
     )
 
 
+def attend_alone_kernel(
+    width_q,
+    proj_ref,
+    cos_ref,
+    sin_ref,
+    cot_ref,
+    out_ref,
+    inner_ref,
+    held,
+    before,
+    back_out,
+    back_in,
+    own_grad,
+    kv_sems,
+    back_sems,
+):
+    rows = proj_ref.shape[0]
+    width_k = (proj_ref.shape[1] - width_q) // 2
+    heads_k = width_k // HD
+    group = width_q // width_k
+    inv_scale = 1.0 / math.sqrt(HD)
+    seqs, seq = lax.axis_size("seq"), lax.axis_index("seq")
+    cosine, sine_part = cos_ref[...], sin_ref[...]
+    for head in range(heads_k):
+        low = head * HD
+        at = slice(low, low + HD)
+        keys = proj_ref[:, width_q + low : width_q + low + HD]
+        held[:, at] = turn(keys, cosine, sine_part, 1.0).astype(jnp.bfloat16)
+        values = proj_ref[:, width_q + width_k + low : width_q + width_k + low + HD]
+        held[:, width_k + low : width_k + low + HD] = values.astype(jnp.bfloat16)
+    greet(("seq",))
+    ahead = pltpu.make_async_remote_copy(
+        src_ref=held,
+        dst_ref=before,
+        send_sem=kv_sems.at[0],
+        recv_sem=kv_sems.at[1],
+        device_id={"seq": seq + 1},
+        device_id_type=MESH,
+    )
+    behind = pltpu.make_async_remote_copy(
+        src_ref=back_out,
+        dst_ref=back_in,
+        send_sem=back_sems.at[0],
+        recv_sem=back_sems.at[1],
+        device_id={"seq": seq - 1},
+        device_id_type=MESH,
+    )
+    has_next, has_last = seq < seqs - 1, seq > 0
+
+    @pl.when(has_next)
+    def _():
+        ahead.start()
+
+    queries = []
+    for head in range(heads_k * group):
+        part = proj_ref[:, head * HD : (head + 1) * HD]
+        queries.append(turn(part, cosine, sine_part, 1.0).astype(jnp.bfloat16))
+
+    @pl.when(has_last)
+    def _():
+        ahead.wait_recv()
+
+    @pl.when(jnp.logical_not(has_last))
+    def _():
+        before[...] = jnp.zeros_like(before)
+
+    query_at = lax.broadcasted_iota(jnp.int32, (rows, rows), 0)
+    key_at = lax.broadcasted_iota(jnp.int32, (rows, rows), 1)
+    masks = (
+        (key_at > query_at + (rows - WINDOW)) & (seq * rows - rows + key_at >= 0),
+        (key_at <= query_at) & (key_at > query_at - WINDOW),
+    )
+    for head in range(heads_k):
+        at = slice(head * HD, (head + 1) * HD)
+        at_value = slice(width_k + head * HD, width_k + (head + 1) * HD)
+        sides = (before, held)
+        key_grads, value_grads = [0.0, 0.0], [0.0, 0.0]
+        for member in range(group):
+            index = head * group + member
+            query = queries[index]
+            cot = cot_ref[:, index * HD : (index + 1) * HD]
+            squashes, terms, slopes = [], [], []
+            for side, mask in zip(sides, masks):
+                squash = jnp.tanh(product(query, side[:, at], 1, 1) * inv_scale / SOFTCAP)
+                squashes.append(squash)
+                terms.append(jnp.where(mask, jnp.exp(SOFTCAP * squash), 0.0))
+                slopes.append(product(cot, side[:, at_value], 1, 1))
+            total = sum(jnp.sum(term, -1, keepdims=True) for term in terms)
+            probs = [term / total for term in terms]
+            delta = sum(
+                jnp.sum(prob * slope, -1, keepdims=True) for prob, slope in zip(probs, slopes)
+            )
+            dquery = 0.0
+            for which in range(2):
+                prob, squash = probs[which], squashes[which]
+                dlogits = (
+                    prob * (slopes[which] - delta) * (1.0 - squash * squash) * inv_scale
+                ).astype(jnp.bfloat16)
+                dquery = dquery + product(dlogits, sides[which][:, at], 1, 0)
+                key_grads[which] = key_grads[which] + product(dlogits, query, 0, 0)
+                value_grads[which] = value_grads[which] + product(
+                    prob.astype(jnp.bfloat16), cot, 0, 0
+                )
+            out_ref[:, index * HD : (index + 1) * HD] = turn(
+                dquery, cosine, sine_part, -1.0
+            ).astype(jnp.bfloat16)
+        back_out[:, at] = key_grads[0].astype(jnp.bfloat16)
+        back_out[:, at_value] = value_grads[0].astype(jnp.bfloat16)
+        own_grad[:, at] = key_grads[1]
+        own_grad[:, at_value] = value_grads[1]
+
+    @pl.when(has_last)
+    def _():
+        behind.start()
+
+    @pl.when(has_next)
+    def _():
+        behind.wait_recv()
+        own_grad[...] += back_in[...].astype(jnp.float32)
+
+    for head in range(heads_k):
+        at = slice(head * HD, (head + 1) * HD)
+        out_ref[:, width_q + head * HD : width_q + (head + 1) * HD] = turn(
+            own_grad[:, at], cosine, sine_part, -1.0
+        ).astype(jnp.bfloat16)
+    out_ref[:, width_q + width_k :] = own_grad[:, width_k:].astype(jnp.bfloat16)
+
+    @pl.when(has_next)
+    def _():
+        ahead.wait_send()
+
+    @pl.when(has_last)
+    def _():
+        behind.wait_send()
+
+    inner = 0.0
+    for low in range(0, out_ref.shape[1], 128):
+        at = slice(low, low + 128)
+        inner = inner + out_ref[:, at].astype(jnp.float32) * proj_ref[:, at]
+    inner = jnp.broadcast_to(jnp.sum(inner, -1, keepdims=True), (rows, 128))
+    inner_ref[...] = inner.T[:8]
+
+
+def attend_alone(projected, cosine, sine_part, cotangent, collective_id):
+    rows, width_q = cotangent.shape
+    width_k = (projected.shape[1] - width_q) // 2
+    return pl.pallas_call(
+        functools.partial(attend_alone_kernel, width_q),
+        out_shape=(
+            jax.ShapeDtypeStruct(projected.shape, jnp.bfloat16),
+            jax.ShapeDtypeStruct((8, rows), jnp.float32),
+        ),
+        in_specs=[pl.BlockSpec(memory_space=pltpu.VMEM)] * 4,
+        out_specs=(pl.BlockSpec(memory_space=pltpu.VMEM),) * 2,
+        scratch_shapes=[
+            pltpu.VMEM((rows, 2 * width_k), jnp.bfloat16),
+            pltpu.VMEM((rows, 2 * width_k), jnp.bfloat16),
+            pltpu.VMEM((rows, 2 * width_k), jnp.bfloat16),
+            pltpu.VMEM((rows, 2 * width_k), jnp.bfloat16),
+            pltpu.VMEM((rows, 2 * width_k), jnp.float32),
+            pltpu.SemaphoreType.DMA((2,)),
+            pltpu.SemaphoreType.DMA((2,)),
+        ],
+        compiler_params=pltpu.CompilerParams(
+            collective_id=collective_id, has_side_effects=True
+        ),
+    )(projected, cosine, sine_part, cotangent)
+
+
+def others_of(axis):
+    count, me = lax.axis_size(axis), lax.axis_index(axis)
+    return [lax.rem(me + hop, count) for hop in range(1, count)]
+
+
+def signal_all(peers):
+    barrier = pltpu.get_barrier_semaphore()
+    for peer in peers:
+        pl.semaphore_signal(barrier, inc=1, device_id=peer, device_id_type=MESH)
+    return barrier
+
+
+def remote(src, dst, send_sem, recv_sem, device):
+    return pltpu.make_async_remote_copy(
+        src_ref=src,
+        dst_ref=dst,
+        send_sem=send_sem,
+        recv_sem=recv_sem,
+        device_id=device,
+        device_id_type=MESH,
+    )
+
+
+def line(axis, far_first):
+    count, me = lax.axis_size(axis), lax.axis_index(axis)
+    order = range(count - 1, 0, -1) if far_first else range(1, count)
+    found = []
+    for index, (hop, step) in enumerate((hop, step) for hop in order for step in (-1, 1)):
+        at = me + step * hop
+        found.append((index, step, at, (at >= 0) & (at < count)))
+    return found
+
+
+def project_kernel(
+    x_ref,
+    gain_ref,
+    wq_ref,
+    wk_ref,
+    wv_ref,
+    proj_ref,
+    w_ref,
+    slabs_ref,
+    rms_ref,
+    turned,
+    every,
+    natural,
+    acc,
+    sent,
+    got,
+    w_send,
+    w_recv,
+    own_sem,
+    x_send,
+    x_recv,
+    f_send,
+    f_recv,
+    r_send,
+    r_recv,
+    s_send,
+    s_recv,
+):
+    seqs, dps, lanes = (lax.axis_size(axis) for axis in ("seq", "dp", "tensor"))
+    seq, dp, lane = (lax.axis_index(axis) for axis in ("seq", "dp", "tensor"))
+    rows, features = x_ref.shape
+    block = wq_ref.shape[0]
+    share = block // lanes
+    mine = pl.ds(pl.multiple_of(lane * share, 16), share)
+    peers = [{axis: other} for axis in ("seq", "dp", "tensor") for other in others_of(axis)]
+    barrier = signal_all(peers)
+    squares = jnp.zeros((rows, 128), jnp.float32)
+    for low in range(0, features, 128):
+        part = x_ref[:, low : low + 128].astype(jnp.float32)
+        squares = squares + part * part
+    inverse = lax.rsqrt(jnp.sum(squares, -1, keepdims=True) / features + EPSILON)
+    rms_ref[...] = jnp.broadcast_to(inverse, rms_ref.shape)
+    pl.semaphore_wait(barrier, len(peers))
+
+    chunks, base = [], 0
+    for ref in (wq_ref, wk_ref, wv_ref):
+        chunks.append([(ref, low, base + low) for low in range(0, ref.shape[1], HD)])
+        base = base + ref.shape[1]
+    chunks = chunks[1] + chunks[2] + chunks[0]
+
+    def w_copy(index, hop, other):
+        ref, low, to = chunks[index]
+        return remote(
+            ref.at[:, low : low + HD],
+            w_ref.at[seq, :, to : to + HD],
+            w_send.at[hop, index],
+            w_recv.at[seq, index],
+            {"seq": other},
+        )
+
+    owns = []
+    for index, (ref, low, to) in enumerate(chunks):
+        owns.append(
+            pltpu.make_async_copy(
+                ref.at[:, low : low + HD], w_ref.at[seq, :, to : to + HD], own_sem.at[index]
+            )
+        )
+        owns[-1].start()
+        for hop, other in enumerate(others_of("seq")):
+            w_copy(index, hop, other).start()
+
+    for low in range(0, features, 128):
+        part = x_ref[:, low : low + 128].astype(jnp.float32)
+        part = (part * inverse * gain_ref[:, low : low + 128]).astype(jnp.bfloat16).T
+        at = low
+        while at < low + 128:
+            index = at // block
+            end = min(low + 128, (index + 1) * block)
+            turned[index // dps, index % dps, at - index * block : end - index * block, :] = part[
+                at - low : end - low
+            ]
+            at = end
+
+    def x_copy(other):
+        return remote(
+            turned.at[:, other, mine],
+            every.at[dp, :, mine],
+            x_send.at[other],
+            x_recv.at[dp],
+            {"dp": other},
+        )
+
+    own_x = pltpu.make_async_copy(turned.at[:, dp], every.at[dp], own_sem.at[len(chunks)])
+    own_x.start()
+    for _, _, other, held in line("dp", True):
+
+        @pl.when(held)
+        def _():
+            x_copy(other).start()
+
+    def f_copy(source, hop, other):
+        return remote(
+            every.at[source, :, mine],
+            every.at[source, :, mine],
+            f_send.at[source, hop],
+            f_recv.at[source, lane],
+            {"tensor": other},
+        )
+
+    def f_arrival(source, other):
+        part = every.at[source, :, pl.ds(pl.multiple_of(other * share, 16), share)]
+        return remote(
+            part, part, f_send.at[source, 0], f_recv.at[source, other], {"tensor": other}
+        )
+
+    for _, _, source, held in line("dp", False):
+
+        @pl.when(held)
+        def _():
+            remote(
+                every.at[source, :, mine],
+                every.at[source, :, mine],
+                x_send.at[source],
+                x_recv.at[source],
+                {"dp": source},
+            ).wait_recv()
+            for hop, other in enumerate(others_of("tensor")):
+                f_copy(source, hop, other).start()
+
+    def partial(source, index):
+        _, _, to = chunks[index]
+        weights = w_ref[:, :, to : to + HD].reshape(seqs * block, HD)
+        return product(natural[source], weights, 1, 0)
+
+    def turn_back(source):
+        natural[source] = every[source].reshape(seqs * block, rows).T
+
+    def r_copy(step, index, which, target):
+        way = 0 if step == -1 else 1
+        return remote(
+            sent.at[index, which],
+            got.at[way, index, target],
+            r_send.at[index, which],
+            r_recv.at[way, index, target],
+            {"dp": dp + step},
+        )
+
+    def upstream(step):
+        return dp < dps - 1 if step == -1 else dp > 0
+
+    def r_arrival(step, index, target):
+        way = 0 if step == -1 else 1
+        remote(
+            got.at[way, index, target],
+            got.at[way, index, target],
+            r_send.at[index, 0],
+            r_recv.at[way, index, target],
+            {"dp": dp},
+        ).wait_recv()
+        acc[...] += got[way, index, target].astype(jnp.float32)
+
+    def finish_chunk(index):
+        _, _, to = chunks[index]
+        acc[...] = partial(dp, index)
+        for step in (-1, 1):
+
+            @pl.when(upstream(step))
+            def _():
+                r_arrival(step, index, dp)
+
+        proj_ref[:, to : to + HD] = acc[...]
+
+    slab_own = pltpu.make_async_copy(
+        every.at[:, seq], slabs_ref.at[seq], own_sem.at[len(chunks) + 1]
+    )
+
+    def s_copy(hop, other):
+        return remote(
+            every.at[:, other], slabs_ref.at[seq], s_send.at[hop], s_recv.at[seq], {"seq": other}
+        )
+
+    for index in range(len(chunks)):
+        owns[index].wait()
+        for other in others_of("seq"):
+            _, _, to = chunks[index]
+            remote(
+                w_ref.at[other, :, to : to + HD],
+                w_ref.at[other, :, to : to + HD],
+                w_send.at[0, index],
+                w_recv.at[other, index],
+                {"seq": other},
+            ).wait_recv()
+        for which, step, target, held in line("dp", True):
+
+            @pl.when(held)
+            def _():
+                if index == 0:
+                    for other in others_of("tensor"):
+                        f_arrival(target, other).wait_recv()
+                    turn_back(target)
+                acc[...] = partial(target, index)
+
+                @pl.when(upstream(step))
+                def _():
+                    r_arrival(step, index, target)
+
+                sent[index, which] = acc[...].astype(jnp.bfloat16)
+                r_copy(step, index, which, target).start()
+
+        if index == 0:
+            own_x.wait()
+            turn_back(dp)
+            slab_own.start()
+            for hop, other in enumerate(others_of("seq")):
+                s_copy(hop, other).start()
+        else:
+            finish_chunk(index - 1)
+    finish_chunk(len(chunks) - 1)
+
+    slab_own.wait()
+    for hop, other in enumerate(others_of("seq")):
+        s_copy(hop, other).wait_send()
+        remote(
+            every.at[:, other], slabs_ref.at[other], s_send.at[hop], s_recv.at[other], {"seq": other}
+        ).wait_recv()
+        for index in range(len(chunks)):
+            w_copy(index, hop, other).wait_send()
+    for which, step, target, held in line("dp", True):
+
+        @pl.when(held)
+        def _():
+            x_copy(target).wait_send()
+            for hop, other in enumerate(others_of("tensor")):
+                f_copy(target, hop, other).wait_send()
+            for index in range(len(chunks)):
+                r_copy(step, index, which, target).wait_send()
+
+
+def project(x, gain, w_query, w_key, w_value, collective_id):
+    seqs, dps, lanes = (lax.axis_size(axis) for axis in ("seq", "dp", "tensor"))
+    rows, features = x.shape
+    block = w_query.shape[0]
+    width = w_query.shape[1] + w_key.shape[1] + w_value.shape[1]
+    count = width // HD
+    hops = 2 * (dps - 1)
+    vmem = pl.BlockSpec(memory_space=pltpu.VMEM)
+    dma = pltpu.SemaphoreType.DMA
+    return pl.pallas_call(
+        project_kernel,
+        out_shape=(
+            jax.ShapeDtypeStruct((rows, width), jnp.float32),
+            jax.ShapeDtypeStruct((seqs, block, width), jnp.bfloat16),
+            jax.ShapeDtypeStruct((seqs, dps, block, rows), jnp.bfloat16),
+            jax.ShapeDtypeStruct((rows, 128), jnp.float32),
+        ),
+        in_specs=[vmem, vmem] + [pl.BlockSpec(memory_space=pl.ANY)] * 3,
+        out_specs=(vmem,) * 4,
+        scratch_shapes=[
+            pltpu.VMEM((seqs, dps, block, rows), jnp.bfloat16),
+            pltpu.VMEM((dps, seqs, block, rows), jnp.bfloat16),
+            pltpu.VMEM((dps, rows, seqs * block), jnp.bfloat16),
+            pltpu.VMEM((rows, HD), jnp.float32),
+            pltpu.VMEM((count, hops, rows, HD), jnp.bfloat16),
+            pltpu.VMEM((2, count, dps, rows, HD), jnp.bfloat16),
+            dma((seqs - 1, count)),
+            dma((seqs, count)),
+            dma((count + 2,)),
+            dma((dps,)),
+            dma((dps,)),
+            dma((dps, lanes - 1)),
+            dma((dps, lanes)),
+            dma((count, hops)),
+            dma((2, count, dps)),
+            dma((seqs - 1,)),
+            dma((seqs,)),
+        ],
+        compiler_params=pltpu.CompilerParams(
+            collective_id=collective_id, has_side_effects=True
+        ),
+    )(x, gain, w_query, w_key, w_value)
+
+
+def split_rows(rows):
+    return max(16, rows // 6 // 16 * 16)
+
+
+def backward_kernel(
+    cut,
+    d_out_ref,
+    w_ref,
+    slabs_ref,
+    inner_ref,
+    rms_ref,
+    x_ref,
+    gain_ref,
+    gq_ref,
+    gk_ref,
+    gv_ref,
+    out_ref,
+    every,
+    grads,
+    final,
+    inners,
+    squares,
+    small,
+    held_sums,
+    x_slab,
+    *rest,
+):
+    seqs, dps, lanes = (lax.axis_size(axis) for axis in ("seq", "dp", "tensor"))
+    seq, dp, lane = (lax.axis_index(axis) for axis in ("seq", "dp", "tensor"))
+    stages = lanes.bit_length() - 1
+    parts, rest = rest[: stages + 1], rest[stages + 1 :]
+    arrived, rest = rest[:stages], rest[stages:]
+    (g_send, g_recv, own_sem, p_send, p_recv, z_send, z_recv, i_send, i_recv) = rest[:9]
+    t_send, t_recv, u_send, u_recv = rest[9:]
+    rows, width = d_out_ref.shape
+    block = w_ref.shape[1]
+    per_slab = seqs * dps // lanes
+    part_width = per_slab * block
+    column_blocks = width // HD
+
+    near = [{"dp": far, "tensor": other} for far in others_of("dp") for other in others_of("tensor")]
+    near = near + [{"tensor": other} for other in others_of("tensor")]
+    mine, blocks = block_peers()
+    near = near + [{"seq": other, "dp": far} for _, other, far in blocks]
+    barrier = signal_all(near)
+    owns = [
+        pltpu.make_async_copy(d_out_ref, every.at[dp, seq], own_sem.at[0]),
+        pltpu.make_async_copy(
+            x_ref.at[:, pl.ds(pl.multiple_of(lane * part_width, 128), part_width)],
+            x_slab,
+            own_sem.at[1],
+        ),
+        pltpu.make_async_copy(inner_ref, inners.at[lane], own_sem.at[2]),
+    ]
+    for own in owns:
+        own.start()
+    pl.semaphore_wait(barrier, len(near))
+
+    order = ("dp", "seq")
+    by_seq = LineGather(order, 0, "seq", "dp", 0, cut, d_out_ref, every, g_send, g_recv)
+    by_dp = LineGather(order, 1, "dp", "seq", cut, rows, d_out_ref, every, g_send, g_recv)
+    me = {"seq": seq, "dp": dp}
+    here = jnp.bool_(True)
+    for gather, axis in ((by_dp, "dp"), (by_dp, "seq"), (by_seq, "seq"), (by_seq, "dp")):
+        for step in (1, -1):
+            gather.send(dict(me), axis, step, here, True)
+    inner_copies = [
+        remote(inner_ref, inners.at[lane], i_send.at[hop], i_recv.at[lane], {"tensor": other})
+        for hop, other in enumerate(others_of("tensor"))
+    ]
+    for copy in inner_copies:
+        copy.start()
+
+    def weight_grad(at, first):
+        def column(index, carry):
+            columns = pl.ds(pl.multiple_of(index * HD, HD), HD)
+            term = product(slabs_ref[at["seq"], at["dp"]], every[at["dp"], at["seq"], :, columns], 1, 0)
+            if first:
+                grads[at["dp"], :, columns] = term
+            else:
+                grads[at["dp"], :, columns] = grads[at["dp"], :, columns] + term
+            return carry
+
+        lax.fori_loop(0, column_blocks, column, 0)
+
+    def square_sum(example):
+        def some(index, total):
+            group = grads[example, pl.ds(pl.multiple_of(index * 16, 16), 16), :]
+            group = group * group
+            group = group[:8] + group[8:]
+            for low in range(0, width, 128):
+                total = total + group[:, low : low + 128]
+            return total
+
+        total = lax.fori_loop(0, block // 16, some, jnp.zeros((8, 128), jnp.float32))
+        squares[example] = total
+
+    bits = [lax.rem(lane // (1 << stage), 2) for stage in range(stages)]
+    sizes = [block >> stage for stage in range(stages + 1)]
+    start = 0
+    for stage in range(stages):
+        start = start + bits[stage] * sizes[stage + 1]
+
+    def half(stage, bit):
+        return pl.ds(pl.multiple_of(bit * sizes[stage + 1], 16), sizes[stage + 1])
+
+    def p_copy(stage, example):
+        return remote(
+            parts[stage].at[example, :, half(stage, 1 - bits[stage])],
+            arrived[stage].at[example],
+            p_send.at[stage, example],
+            p_recv.at[stage, example],
+            {"tensor": lane + (1 - 2 * bits[stage]) * (1 << stage)},
+        )
+
+    def z_target(part):
+        index = part * dps + dp
+        return index // per_slab, lax.rem(index, per_slab)
+
+    def z_copy(example, part):
+        to, slot = z_target(part)
+        return remote(
+            parts[stages].at[example, part],
+            final.at[slot, pl.ds(pl.multiple_of(start, 16), sizes[stages])],
+            z_send.at[example, part],
+            z_recv.at[slot, lane],
+            {"tensor": to, "dp": example},
+        )
+
+    def z_own(example, part):
+        _, slot = z_target(part)
+        return pltpu.make_async_copy(
+            parts[stages].at[example, part],
+            final.at[slot, pl.ds(pl.multiple_of(start, 16), sizes[stages])],
+            z_recv.at[slot, lane],
+        )
+
+    def z_is_own(example, part):
+        to, _ = z_target(part)
+        return (to == lane) & (example == dp)
+
+    def advance(stage, example):
+        if stage == 0:
+            for part in range(seqs):
+                parts[0][example, part] = product(
+                    w_ref[part], every[example, seq], 1, 1
+                ).astype(jnp.bfloat16)
+        else:
+            p_copy(stage - 1, example).wait_recv()
+            kept = parts[stage - 1][example, :, half(stage - 1, bits[stage - 1])]
+            added = arrived[stage - 1][example]
+            parts[stage][example] = (
+                kept.astype(jnp.float32) + added.astype(jnp.float32)
+            ).astype(jnp.bfloat16)
+        if stage < stages:
+            p_copy(stage, example).start()
+        else:
+            for part in range(seqs):
+
+                @pl.when(z_is_own(example, part))
+                def _():
+                    z_own(example, part).start()
+
+                @pl.when(jnp.logical_not(z_is_own(example, part)))
+                def _():
+                    z_copy(example, part).start()
+
+    groups = [[(dp, None)]] + [
+        [
+            (dp - step * hop, (dp - step * hop >= 0) & (dp - step * hop < dps))
+            for step in (1, -1)
+        ]
+        for hop in range(1, dps)
+    ]
+
+    def each(hop, action):
+        for example, held in groups[hop]:
+            if held is None:
+                action(example)
+            else:
+
+                @pl.when(held)
+                def _():
+                    action(example)
+
+    def spread(hop):
+        column = []
+        for example, held in groups[hop]:
+            column.append(({**me, "dp": example}, here if held is None else held))
+        found = []
+        for base, held_base in column:
+            for far in range(1, seqs):
+                for step in (1, -1):
+                    at = {**base, "seq": seq - step * far}
+                    held = held_base & by_dp.inside("seq", at["seq"])
+                    by_dp.receive(at, held)
+                    by_dp.send(at, "seq", step, held)
+                    found.append((at, held))
+        for at, held in found:
+
+            @pl.when(held)
+            def _():
+                weight_grad(at, False)
+
+        each(hop, square_sum)
+
+    base_columns = [(dict(me), here)]
+    for hop in range(1, seqs):
+        for step in (1, -1):
+            at = {**me, "seq": seq - step * hop}
+            held = by_seq.inside("seq", at["seq"])
+            by_seq.receive(at, held)
+            by_seq.send(at, "seq", step, held)
+            for way in (1, -1):
+                by_seq.send(at, "dp", way, held)
+            base_columns.append((at, held))
+    owns[0].wait()
+    each(0, functools.partial(advance, 0))
+    each(0, lambda example: weight_grad({**me, "dp": example}, True))
+    for hop in range(1, dps):
+        for step in (1, -1):
+            at = {**me, "dp": dp - step * hop}
+            held = by_dp.inside("dp", at["dp"])
+            by_dp.receive(at, held)
+            by_dp.send(at, "dp", step, held)
+            for way in (1, -1):
+                by_dp.send(at, "seq", way, held)
+        for base, held_base in base_columns:
+            for step in (1, -1):
+                at = {**base, "dp": dp - step * hop}
+                held = held_base & by_seq.inside("dp", at["dp"])
+                by_seq.receive(at, held)
+                by_seq.send(at, "dp", step, held)
+        each(hop, functools.partial(advance, 0))
+        for stage in range(1, stages + 1):
+            if 0 <= hop - stage:
+                each(hop - stage, functools.partial(advance, stage))
+        each(hop, lambda example: weight_grad({**me, "dp": example}, True))
+        spread(hop - 1)
+    for late in range(1, stages + 1):
+        for stage in range(late, stages + 1):
+            if 0 <= dps - 1 + late - stage < dps:
+                each(dps - 1 + late - stage, functools.partial(advance, stage))
+        if late == 1:
+            spread(dps - 1)
+            for example in range(dps):
+                small[example : example + 1, :] = jnp.sum(squares[example], 0, keepdims=True)
+            own_sum = pltpu.make_async_copy(small, held_sums.at[lane, mine], own_sem.at[3])
+            own_sum.start()
+            sums = [
+                remote(
+                    small,
+                    held_sums.at[lane, mine],
+                    t_send.at[hop],
+                    t_recv.at[mine],
+                    {"seq": other, "dp": far},
+                )
+                for hop, (_, other, far) in enumerate(blocks)
+            ]
+            for copy in sums:
+                copy.start()
+
+    for hop, (index, other, far) in enumerate(blocks):
+        remote(
+            small,
+            held_sums.at[lane, index],
+            t_send.at[hop],
+            t_recv.at[index],
+            {"seq": other, "dp": far},
+        ).wait_recv()
+    own_sum.wait()
+    wide = [
+        remote(
+            held_sums.at[lane],
+            held_sums.at[lane],
+            u_send.at[hop],
+            u_recv.at[lane],
+            {"tensor": other},
+        )
+        for hop, other in enumerate(others_of("tensor"))
+    ]
+    for copy in wide:
+        copy.start()
+
+    owns[1].wait()
+    owns[2].wait()
+    for hop, other in enumerate(others_of("tensor")):
+        remote(
+            inner_ref, inners.at[other], i_send.at[hop], i_recv.at[other], {"tensor": other}
+        ).wait_recv()
+    total = inners[0]
+    for other in range(1, lanes):
+        total = total + inners[other]
+    total = jnp.broadcast_to(total[:1], (128, rows)).T
+    inverse = rms_ref[...]
+    mean = total * inverse * inverse / x_ref.shape[1]
+    for slot in range(per_slab):
+        for other in range(lanes):
+            where, turn_start = other, 0
+            for stage in range(stages):
+                turn_start = turn_start + (where >> stage) % 2 * sizes[stage + 1]
+            piece = final.at[slot, turn_start : turn_start + sizes[stages]]
+            remote(
+                piece, piece, z_send.at[0, 0], z_recv.at[slot, other], {"tensor": lane}
+            ).wait_recv()
+    for low in range(0, part_width, 128):
+        pieces = []
+        at = low
+        while at < low + 128:
+            slot = at // block
+            end = min(low + 128, (slot + 1) * block)
+            pieces.append(final[slot, at - slot * block : end - slot * block, :])
+            at = end
+        part = pieces[0] if len(pieces) == 1 else jnp.concatenate(pieces, 0)
+        part = part.astype(jnp.float32).T
+        gain = gain_ref[:, pl.ds(pl.multiple_of(lane * part_width + low, 128), 128)]
+        scaled = part * gain
+        out_ref[:, low : low + 128] = (
+            inverse * scaled - x_slab[:, low : low + 128].astype(jnp.float32) * mean
+        ).astype(jnp.bfloat16)
+
+    for hop, other in enumerate(others_of("tensor")):
+        remote(
+            held_sums.at[other],
+            held_sums.at[other],
+            u_send.at[hop],
+            u_recv.at[other],
+            {"tensor": other},
+        ).wait_recv()
+    square = jnp.sum(jnp.sum(held_sums[...], (0, 1)), -1, keepdims=True)
+    grad_rms = jnp.sqrt(square / (D * (H + 2 * KVH) * HD) + EPSILON)
+    factor = CLIP_BOUND / jnp.maximum(grad_rms, CLIP_BOUND)
+    base = 0
+    for ref in (gq_ref, gk_ref, gv_ref):
+        for low in range(0, ref.shape[1], 128):
+            clipped = factor[0:1] * grads[0, :, base + low : base + low + 128]
+            for example in range(1, dps):
+                clipped = clipped + factor[example : example + 1] * (
+                    grads[example, :, base + low : base + low + 128]
+                )
+            ref[:, low : low + 128] = clipped
+        base = base + ref.shape[1]
+
+    by_seq.finish()
+    by_dp.finish()
+    for copy in inner_copies + sums + wide:
+        copy.wait_send()
+
+    def drain(example):
+        for stage in range(stages):
+            p_copy(stage, example).wait_send()
+        for part in range(seqs):
+
+            @pl.when(jnp.logical_not(z_is_own(example, part)))
+            def _():
+                z_copy(example, part).wait_send()
+
+    for hop in range(dps):
+        each(hop, drain)
+
+
+def backward(d_out, weights, slabs, inner, rms, x, gain, widths, collective_id):
+    seqs, dps, lanes = (lax.axis_size(axis) for axis in ("seq", "dp", "tensor"))
+    rows, width = d_out.shape
+    block = weights.shape[1]
+    features = x.shape[1]
+    stages = lanes.bit_length() - 1
+    per_slab = seqs * dps // lanes
+    vmem = pl.BlockSpec(memory_space=pltpu.VMEM)
+    dma = pltpu.SemaphoreType.DMA
+    count = seqs * dps
+    return pl.pallas_call(
+        functools.partial(backward_kernel, split_rows(rows)),
+        out_shape=tuple(jax.ShapeDtypeStruct((block, size), jnp.float32) for size in widths)
+        + (jax.ShapeDtypeStruct((rows, features // lanes), jnp.bfloat16),),
+        in_specs=[vmem] * 5 + [pl.BlockSpec(memory_space=pl.ANY), vmem],
+        out_specs=(vmem,) * 4,
+        scratch_shapes=[
+            pltpu.VMEM((dps, seqs, rows, width), jnp.bfloat16),
+            pltpu.VMEM((dps, block, width), jnp.float32),
+            pltpu.VMEM((per_slab, block, rows), jnp.bfloat16),
+            pltpu.VMEM((lanes,) + inner.shape, jnp.float32),
+            pltpu.VMEM((dps, 8, 128), jnp.float32),
+            pltpu.VMEM((dps, 128), jnp.float32),
+            pltpu.VMEM((lanes, count, dps, 128), jnp.float32),
+            pltpu.VMEM((rows, features // lanes), jnp.bfloat16),
+        ]
+        + [
+            pltpu.VMEM((dps, seqs, block >> stage, rows), jnp.bfloat16)
+            for stage in range(stages + 1)
+        ]
+        + [
+            pltpu.VMEM((dps, seqs, block >> (stage + 1), rows), jnp.bfloat16)
+            for stage in range(stages)
+        ]
+        + [
+            dma((2, 4, seqs, dps)),
+            dma((2, seqs, dps)),
+            dma((4,)),
+            dma((stages, dps)),
+            dma((stages, dps)),
+            dma((dps, seqs)),
+            dma((per_slab, lanes)),
+            dma((lanes - 1,)),
+            dma((lanes,)),
+            dma((count - 1,)),
+            dma((count,)),
+            dma((lanes - 1,)),
+            dma((lanes,)),
+        ],
+        compiler_params=pltpu.CompilerParams(
+            collective_id=collective_id, has_side_effects=True
+        ),
+    )(d_out, weights, slabs, inner, rms, x, gain)
+
+
+def split_local(inputs, w_query, w_key, w_value, norm_gain, attn_grad):
+    x, gain = inputs[0], norm_gain[None, :]
+    rows = x.shape[0]
+    projected, weights, slabs, rms = project(x, gain, w_query, w_key, w_value, 0)
+    start_row = lax.axis_index("seq") * rows
+    cosine, sine_part = angles(start_row + jnp.arange(rows, dtype=jnp.int32), HD)
+    d_out, inner = attend_alone(projected, cosine[:, 0], sine_part[:, 0], attn_grad[0], 3)
+    widths = (w_query.shape[1], w_key.shape[1], w_value.shape[1])
+    grad_query, grad_key, grad_value, input_grad = backward(
+        d_out, weights, slabs, inner, rms, x, gain, widths, 2
+    )
+    return grad_query, grad_key, grad_value, input_grad[None]
+
+
+def local(*args):
+    inputs, w_query = args[:2]
+    seqs, dps, lanes = (lax.axis_size(axis) for axis in ("seq", "dp", "tensor"))
+    block = w_query.shape[0]
+    aligned = block % (16 * lanes) == 0 and inputs.shape[1] % 128 == 0
+    aligned = aligned and (block * seqs * dps // lanes) % 128 == 0
+    even = lanes & (lanes - 1) == 0 and seqs * dps % lanes == 0
+    if aligned and even and min(seqs, dps, lanes) > 1:
+        return split_local(*args)
+    return gathered_local(*args)
+
+
 def solution(mesh):
     return jax.shard_map(
         local,

time: 224 us -> 166 us (0.74)
  matrix products: 23.6 us -> 0 us
  other arithmetic: 18.6 us -> 1.25 us
  Pallas kernels: 172 us -> 158 us
  local copies, waits for them, and re-layouts: 8.73 us -> 5.91 us
    dot_general x10 -> x0, matrix products: 23.6 us -> none  [the longest x8 10.1 us: local(): jnp.dot(slabs[(example * seqs + s) % lanes, (example * seqs + s) // lanes...]
    pallas_call x4 -> x3, Pallas kernels: 172 us -> 158 us  [the longest x1 72.4 us: project(): pl.pallas_call(project_kernel, out_shape=(jax.ShapeDtypeStruct((rows, wid...]
    add x1 -> x0, other arithmetic: 5.95 us -> none  [local(): clipped = sum((factor[example] * grads[example] for example in range(dps)))]
    reduce_sum x3 -> x0, other arithmetic: 3.88 us -> none  [the longest x1 2.02 us: local(): inverse_rms = lax.rsqrt(jnp.mean(widened * widened, -1) + EPSILON)]
    transpose x1 -> x0, local copies, waits for them, and re-layouts: 3.83 us -> none  [local(): normed.T.reshape(seqs, dps, rows_w, row_count)]
    unnamed x16 -> x10, local copies, waits for them, and re-layouts: 1.62 us -> 4.58 us
    another operation x1 -> x0, other arithmetic: 2.56 us -> none  [local(): squares = jnp.stack([jnp.sum(grad * grad) for grad in grads])]
    slice x3 -> x0, local copies, waits for them, and re-layouts: 2.54 us -> none  [the longest x1 1.01 us: local(): clipped[:, :width_q]]
where the time goes in v1:
time: 166 us
  Pallas kernels  158 us (95%)
  local copies, waits for them, and re-layouts  5.91 us (4%)
    pallas_call x1, Pallas kernels, project(): pl.pallas_call(project_kernel, out_shape=(jax.ShapeDtypeStruct((rows, wid...  72.4 us
    pallas_call x1, Pallas kernels, backward(): pl.pallas_call(functools.partial(backward_kernel, split_rows(rows)), out_...  66.6 us
    pallas_call x1, Pallas kernels, attend_alone(): pl.pallas_call(functools.partial(attend_alone_kernel, width_q), out_shape...  18.9 us
    unnamed x10, local copies, waits for them, and re-layouts  4.58 us

profile of v1, /device:TPU:0, one launch (start us, length us, event | category | flops | bytes accessed | tf_op | source)
XLA Modules:
  0.0 165.7 jit_solution(13666242547333144367)
XLA Ops:
  0.7 1.3 broadcast_in_dim.8.gain_ref
  2.0 1.2 multiply_sine_fusion
  3.2 72.4 %shard_map.93 = (f32[256,1024]{1,0:T(8,128)}, bf16[2,448,1024]{2,1,0:T(8,128)(2,1)}, bf16[2,4,448,256]{3,2,1,0:T(8,128)(2,1)}, f32[256,128]{1,0:T(8,128)}) custom-call(bf16[256,3584]{1,0:T(8,128)(2,1)} %bitcast.3, f32[1,3584]{1,0:T(1,128)} %broadcast_in_dim.8.gain_ref, bf16[448,512]{1,0:T(8,128)(2,1)} %wq_ref.1, bf16[448,256]{1,0:T(8,128)(2,1)} %wk_ref.1, ...), custom_call_target="tpu_custom_call" | custom-call | tf_op jit(solution)/shard_map/pallas_call | solution.py:1151
  75.6 18.9 %shard_map.94 = (bf16[256,1024]{1,0:T(8,128)(2,1)}, f32[8,256]{1,0:T(8,128)}) custom-call(f32[256,1024]{1,0:T(8,128)} %get-tuple-element.14.proj_ref, f32[256,128]{1,0:T(8,128)} %get-tuple-element.25.cos_ref, f32[256,128]{1,0:T(8,128)} %get-tuple-element.24.sin_ref, bf16[256,512]{1,0:T(8,128)(2,1)} %bitcast.6), custom_call_target="tpu_custom_call" | custom-call | tf_op jit(solution)/shard_map/pallas_call | solution.py:848
  94.5 66.6 %shard_map.95 = (f32[448,512]{1,0:T(8,128)}, f32[448,256]{1,0:T(8,128)}, f32[448,256]{1,0:T(8,128)}, bf16[256,896]{1,0:T(8,128)(2,1)}) custom-call(bf16[256,1024]{1,0:T(8,128)(2,1)} %get-tuple-element.15.d_out_ref, bf16[2,448,1024]{2,1,0:T(8,128)(2,1)} %get-tuple-element.16.w_ref, bf16[2,4,448,256]{3,2,1,0:T(8,128)(2,1)} %get-tuple-element.17.slabs_ref, ...), custom_call_target="tpu_custom_call" | custom-call | tf_op jit(solution)/shard_map/pallas_call | solution.py:1557
  161.1 0.0 copy-start.2
  161.1 0.0 copy-start.1
  161.1 0.0 copy-start
  161.2 2.3 %copy.14 = f32[448,512]{1,0:T(8,128)} copy(f32[448,512]{1,0:T(8,128)} %get-tuple-element.30) | data formatting | bytes 1835008
  163.4 0.0 copy-done.2
  163.4 0.8 copy.15
  164.2 0.0 copy-done.1
  164.2 0.8 copy.16
  165.0 0.0 copy-done
  165.0 0.8 copy.17
  (2 shorter events, 0.0 us)
Async XLA Ops:
  161.1 2.3 %copy-start.2 = (f32[448,256]{1,0:T(8,128)S(1)}, f32[448,256]{1,0:T(8,128)}, u32[]{:S(2)}) copy-start(f32[448,256]{1,0:T(8,128)} %get-tuple-element.31) | copy-start | bytes 1376260
  161.1 3.1 %copy-start.1 = (f32[448,256]{1,0:T(8,128)S(1)}, f32[448,256]{1,0:T(8,128)}, u32[]{:S(2)}) copy-start(f32[448,256]{1,0:T(8,128)} %get-tuple-element.32) | copy-start | bytes 1376260
  161.1 3.8 %copy-start = (bf16[256,896]{1,0:T(8,128)(2,1)S(1)}, bf16[256,896]{1,0:T(8,128)(2,1)}, u32[]{:S(2)}) copy-start(bf16[256,896]{1,0:T(8,128)(2,1)} %get-tuple-element.23) | copy-start | bytes 1376260

commit v2 on v1

--- a/solution.py
+++ b/solution.py
@@ -895,10 +895,27 @@
     count, me = lax.axis_size(axis), lax.axis_index(axis)
     order = range(count - 1, 0, -1) if far_first else range(1, count)
     found = []
-    for index, (hop, step) in enumerate((hop, step) for hop in order for step in (-1, 1)):
-        at = me + step * hop
-        found.append((index, step, at, (at >= 0) & (at < count)))
+    for hop in order:
+        for which, step in enumerate((-1, 1)):
+            at = me + step * hop
+            found.append((2 * hop - 2 + which, step, at, (at >= 0) & (at < count)))
     return found
+
+
+def halvings(block):
+    lanes, lane = lax.axis_size("tensor"), lax.axis_index("tensor")
+    stages = lanes.bit_length() - 1
+    bits = [lax.rem(lane // (1 << stage), 2) for stage in range(stages)]
+    return bits, [block >> stage for stage in range(stages + 1)]
+
+
+def lane_start(lane, block):
+    stages = lax.axis_size("tensor").bit_length() - 1
+    return sum(((lane >> stage) & 1) * (block >> (stage + 1)) for stage in range(stages))
+
+
+def partner(bits, stage):
+    return {"tensor": lax.axis_index("tensor") + (1 - 2 * bits[stage]) * (1 << stage)}
 
 
 def project_kernel(
@@ -933,8 +950,14 @@
     seq, dp, lane = (lax.axis_index(axis) for axis in ("seq", "dp", "tensor"))
     rows, features = x_ref.shape
     block = wq_ref.shape[0]
-    share = block // lanes
-    mine = pl.ds(pl.multiple_of(lane * share, 16), share)
+    bits, sizes = halvings(block)
+    stages = len(bits)
+
+    def region(stage):
+        start = sum(bits[level] * sizes[level + 1] for level in range(stage + 1))
+        return pl.ds(pl.multiple_of(start, 16), sizes[stage + 1])
+
+    mine = region(stages - 1)
     peers = [{axis: other} for axis in ("seq", "dp", "tensor") for other in others_of(axis)]
     barrier = signal_all(peers)
     squares = jnp.zeros((rows, 128), jnp.float32)
@@ -974,7 +997,7 @@
 
     for low in range(0, features, 128):
         part = x_ref[:, low : low + 128].astype(jnp.float32)
-        part = (part * inverse * gain_ref[:, low : low + 128]).astype(jnp.bfloat16).T
+        part = (part * inverse * gain_ref[low : low + 128][None, :]).astype(jnp.bfloat16).T
         at = low
         while at < low + 128:
             index = at // block
@@ -995,40 +1018,21 @@
 
     own_x = pltpu.make_async_copy(turned.at[:, dp], every.at[dp], own_sem.at[len(chunks)])
     own_x.start()
-    for _, _, other, held in line("dp", True):
+    for _, _, other, held in line("dp", False):
 
         @pl.when(held)
         def _():
             x_copy(other).start()
 
-    def f_copy(source, hop, other):
+    def f_copy(stage, source):
+        part = every.at[source, :, region(stage)]
         return remote(
-            every.at[source, :, mine],
-            every.at[source, :, mine],
-            f_send.at[source, hop],
-            f_recv.at[source, lane],
-            {"tensor": other},
-        )
-
-    def f_arrival(source, other):
-        part = every.at[source, :, pl.ds(pl.multiple_of(other * share, 16), share)]
-        return remote(
-            part, part, f_send.at[source, 0], f_recv.at[source, other], {"tensor": other}
-        )
-
-    for _, _, source, held in line("dp", False):
-
-        @pl.when(held)
-        def _():
-            remote(
-                every.at[source, :, mine],
-                every.at[source, :, mine],
-                x_send.at[source],
-                x_recv.at[source],
-                {"dp": source},
-            ).wait_recv()
-            for hop, other in enumerate(others_of("tensor")):
-                f_copy(source, hop, other).start()
+            part, part, f_send.at[stage, source], f_recv.at[stage, source], partner(bits, stage)
+        )
+
+    def x_arrival(source):
+        part = every.at[source, :, mine]
+        remote(part, part, x_send.at[source], x_recv.at[source], {"dp": source}).wait_recv()
 
     def partial(source, index):
         _, _, to = chunks[index]
@@ -1082,7 +1086,7 @@
             every.at[:, other], slabs_ref.at[seq], s_send.at[hop], s_recv.at[seq], {"seq": other}
         )
 
-    for index in range(len(chunks)):
+    def weights_ready(index):
         owns[index].wait()
         for other in others_of("seq"):
             _, _, to = chunks[index]
@@ -1093,31 +1097,64 @@
                 w_recv.at[other, index],
                 {"seq": other},
             ).wait_recv()
+
+    def pass_on(which, step, index, target):
+        acc[...] = partial(target, index)
+
+        @pl.when(upstream(step))
+        def _():
+            r_arrival(step, index, target)
+
+        sent[index, which] = acc[...].astype(jnp.bfloat16)
+        r_copy(step, index, which, target).start()
+
+    def phase(number, which, step, source):
+        if number == 0:
+            x_arrival(source)
+        else:
+            f_copy(stages - number, source).wait_recv()
+        if number < stages:
+            f_copy(stages - 1 - number, source).start()
+        else:
+            turn_back(source)
+
+            @pl.when(jnp.logical_not(upstream(step)))
+            def _():
+                pass_on(which, step, 0, source)
+
+    nearest = line("dp", False)
+    for tick in range(dps - 1 + stages):
+        if tick == stages:
+            weights_ready(0)
+        for number in range(stages + 1):
+            hop = tick - number
+            if 0 <= hop < dps - 1:
+                for which, step, source, held in nearest[2 * hop : 2 * hop + 2]:
+
+                    @pl.when(held)
+                    def _():
+                        phase(number, which, step, source)
+
+    for which, step, target, held in line("dp", True):
+
+        @pl.when(held & upstream(step))
+        def _():
+            pass_on(which, step, 0, target)
+
+    own_x.wait()
+    turn_back(dp)
+    slab_own.start()
+    for hop, other in enumerate(others_of("seq")):
+        s_copy(hop, other).start()
+    for index in range(1, len(chunks)):
+        weights_ready(index)
         for which, step, target, held in line("dp", True):
 
             @pl.when(held)
             def _():
-                if index == 0:
-                    for other in others_of("tensor"):
-                        f_arrival(target, other).wait_recv()
-                    turn_back(target)
-                acc[...] = partial(target, index)
-
-                @pl.when(upstream(step))
-                def _():
-                    r_arrival(step, index, target)
-
-                sent[index, which] = acc[...].astype(jnp.bfloat16)
-                r_copy(step, index, which, target).start()
-
-        if index == 0:
-            own_x.wait()
-            turn_back(dp)
-            slab_own.start()
-            for hop, other in enumerate(others_of("seq")):
-                s_copy(hop, other).start()
-        else:
-            finish_chunk(index - 1)
+                pass_on(which, step, index, target)
+
+        finish_chunk(index - 1)
     finish_chunk(len(chunks) - 1)
 
     slab_own.wait()
@@ -1133,8 +1170,8 @@
         @pl.when(held)
         def _():
             x_copy(target).wait_send()
-            for hop, other in enumerate(others_of("tensor")):
-                f_copy(target, hop, other).wait_send()
+            for stage in range(stages):
+                f_copy(stage, target).wait_send()
             for index in range(len(chunks)):
                 r_copy(step, index, which, target).wait_send()
 
@@ -1145,7 +1182,7 @@
     block = w_query.shape[0]
     width = w_query.shape[1] + w_key.shape[1] + w_value.shape[1]
     count = width // HD
-    hops = 2 * (dps - 1)
+    hops, stages = 2 * (dps - 1), lanes.bit_length() - 1
     vmem = pl.BlockSpec(memory_space=pltpu.VMEM)
     dma = pltpu.SemaphoreType.DMA
     return pl.pallas_call(
@@ -1170,8 +1207,8 @@
             dma((count + 2,)),
             dma((dps,)),
             dma((dps,)),
-            dma((dps, lanes - 1)),
-            dma((dps, lanes)),
+            dma((stages, dps)),
+            dma((stages, dps)),
             dma((count, hops)),
             dma((2, count, dps)),
             dma((seqs - 1,)),
@@ -1280,11 +1317,8 @@
         total = lax.fori_loop(0, block // 16, some, jnp.zeros((8, 128), jnp.float32))
         squares[example] = total
 
-    bits = [lax.rem(lane // (1 << stage), 2) for stage in range(stages)]
-    sizes = [block >> stage for stage in range(stages + 1)]
-    start = 0
-    for stage in range(stages):
-        start = start + bits[stage] * sizes[stage + 1]
+    bits, sizes = halvings(block)
+    start = sum(bits[stage] * sizes[stage + 1] for stage in range(stages))
 
     def half(stage, bit):
         return pl.ds(pl.multiple_of(bit * sizes[stage + 1], 16), sizes[stage + 1])
@@ -1295,7 +1329,7 @@
             arrived[stage].at[example],
             p_send.at[stage, example],
             p_recv.at[stage, example],
-            {"tensor": lane + (1 - 2 * bits[stage]) * (1 << stage)},
+            partner(bits, stage),
         )
 
     def z_target(part):
@@ -1481,9 +1515,7 @@
     mean = total * inverse * inverse / x_ref.shape[1]
     for slot in range(per_slab):
         for other in range(lanes):
-            where, turn_start = other, 0
-            for stage in range(stages):
-                turn_start = turn_start + (where >> stage) % 2 * sizes[stage + 1]
+            turn_start = lane_start(other, block)
             piece = final.at[slot, turn_start : turn_start + sizes[stages]]
             remote(
                 piece, piece, z_send.at[0, 0], z_recv.at[slot, other], {"tensor": lane}
@@ -1498,7 +1530,7 @@
             at = end
         part = pieces[0] if len(pieces) == 1 else jnp.concatenate(pieces, 0)
         part = part.astype(jnp.float32).T
-        gain = gain_ref[:, pl.ds(pl.multiple_of(lane * part_width + low, 128), 128)]
+        gain = gain_ref[pl.ds(pl.multiple_of(lane * part_width + low, 128), 128)][None, :]
         scaled = part * gain
         out_ref[:, low : low + 128] = (
             inverse * scaled - x_slab[:, low : low + 128].astype(jnp.float32) * mean
@@ -1600,7 +1632,7 @@
 
 
 def split_local(inputs, w_query, w_key, w_value, norm_gain, attn_grad):
-    x, gain = inputs[0], norm_gain[None, :]
+    x, gain = inputs[0], norm_gain
     rows = x.shape[0]
     projected, weights, slabs, rms = project(x, gain, w_query, w_key, w_value, 0)
     start_row = lax.axis_index("seq") * rows

time: 166 us -> 156 us (0.940)
  Pallas kernels: 158 us -> 149 us
    pallas_call x1, Pallas kernels: 72.4 us -> 67.3 us  [project(): pl.pallas_call(project_kernel, out_shape=(jax.ShapeDtypeStruct((rows, wid...]
    pallas_call x1, Pallas kernels: 18.9 us -> 16.2 us  [attend_alone(): pl.pallas_call(functools.partial(attend_alone_kernel, width_q), out_shape...]
where the time goes in v2:
time: 156 us
  Pallas kernels  149 us (96%)
  local copies, waits for them, and re-layouts  4.58 us (3%)
    pallas_call x1, Pallas kernels, project(): pl.pallas_call(project_kernel, out_shape=(jax.ShapeDtypeStruct((rows, wid...  67.3 us
    pallas_call x1, Pallas kernels, backward(): pl.pallas_call(functools.partial(backward_kernel, split_rows(rows)), out_...  66 us
    pallas_call x1, Pallas kernels, attend_alone(): pl.pallas_call(functools.partial(attend_alone_kernel, width_q), out_shape...  16.2 us
    unnamed x10, local copies, waits for them, and re-layouts  4.58 us

profile of v2, /device:TPU:0, one launch (start us, length us, event | category | flops | bytes accessed | tf_op | source)
XLA Modules:
  0.0 155.9 jit_solution(10794254176103324547)
XLA Ops:
  0.7 1.2 multiply_sine_fusion
  1.9 67.3 %shard_map.93 = (f32[256,1024]{1,0:T(8,128)}, bf16[2,448,1024]{2,1,0:T(8,128)(2,1)}, bf16[2,4,448,256]{3,2,1,0:T(8,128)(2,1)}, f32[256,128]{1,0:T(8,128)}) custom-call(bf16[256,3584]{1,0:T(8,128)(2,1)} %bitcast.3, f32[3584]{0:T(1024)} %gain_ref.3, bf16[448,512]{1,0:T(8,128)(2,1)} %wq_ref.1, bf16[448,256]{1,0:T(8,128)(2,1)} %wk_ref.1, bf16[448,256]{1,0:T(8,128)(2,1)} %wv_ref.1), custom_call_target="tpu_custom_call" | custom-call | tf_op jit(solution)/shard_map/pallas_call | solution.py:1188
  69.2 16.2 %shard_map.94 = (bf16[256,1024]{1,0:T(8,128)(2,1)}, f32[8,256]{1,0:T(8,128)}) custom-call(f32[256,1024]{1,0:T(8,128)} %get-tuple-element.14.proj_ref, f32[256,128]{1,0:T(8,128)} %get-tuple-element.25.cos_ref, f32[256,128]{1,0:T(8,128)} %get-tuple-element.24.sin_ref, bf16[256,512]{1,0:T(8,128)(2,1)} %bitcast.6), custom_call_target="tpu_custom_call" | custom-call | tf_op jit(solution)/shard_map/pallas_call | solution.py:848
  85.4 66.0 %shard_map.95 = (f32[448,512]{1,0:T(8,128)}, f32[448,256]{1,0:T(8,128)}, f32[448,256]{1,0:T(8,128)}, bf16[256,896]{1,0:T(8,128)(2,1)}) custom-call(bf16[256,1024]{1,0:T(8,128)(2,1)} %get-tuple-element.15.d_out_ref, bf16[2,448,1024]{2,1,0:T(8,128)(2,1)} %get-tuple-element.16.w_ref, bf16[2,4,448,256]{3,2,1,0:T(8,128)(2,1)} %get-tuple-element.17.slabs_ref, ...), custom_call_target="tpu_custom_call" | custom-call | tf_op jit(solution)/shard_map/pallas_call | solution.py:1589
  151.3 0.0 copy-start.2
  151.3 0.0 copy-start.1
  151.4 0.0 copy-start
  151.4 2.3 %copy.14 = f32[448,512]{1,0:T(8,128)} copy(f32[448,512]{1,0:T(8,128)} %get-tuple-element.30) | data formatting | bytes 1835008
  153.6 0.0 copy-done.2
  153.6 0.8 copy.15
  154.4 0.0 copy-done.1
  154.4 0.8 copy.16
  155.2 0.0 copy-done
  155.2 0.8 copy.17
  (2 shorter events, 0.0 us)
Async XLA Ops:
  151.3 2.3 %copy-start.2 = (f32[448,256]{1,0:T(8,128)S(1)}, f32[448,256]{1,0:T(8,128)}, u32[]{:S(2)}) copy-start(f32[448,256]{1,0:T(8,128)} %get-tuple-element.31) | copy-start | bytes 1376260
  151.3 3.1 %copy-start.1 = (f32[448,256]{1,0:T(8,128)S(1)}, f32[448,256]{1,0:T(8,128)}, u32[]{:S(2)}) copy-start(f32[448,256]{1,0:T(8,128)} %get-tuple-element.32) | copy-start | bytes 1376260
  151.4 3.8 %copy-start = (bf16[256,896]{1,0:T(8,128)(2,1)S(1)}, bf16[256,896]{1,0:T(8,128)(2,1)}, u32[]{:S(2)}) copy-start(bf16[256,896]{1,0:T(8,128)(2,1)} %get-tuple-element.23) | copy-start | bytes 1376260
